TPU v7x, 512 devices: a whole 4x4x16 slice. The times are simulated.
512 devices in a mesh: expert: 8 (over x_lo, y), shard: 64 (over x_hi, z, core).
Axes of the slice: x: 4 (x_hi: 2, x_lo: 2; x = x_hi * 2 + x_lo), y: 4, z: 16, core: 2. Of those that a mesh axis runs over, the one named last changes fastest.
Arguments:
- fast_weights: bfloat16 [8, 64, 1, 64, 14336], P('expert', 'shard'), may hold values from -0.25 to 0.25
- slow_weights: float32 [8, 1, 64, 14336], P('expert', None, None, 'shard'), may hold values from -0.09375 to 0.09375
- step_counts: int32 [8, 64], P('expert', 'shard'), may hold values from 1 to 16
- token_counts: int32 [8, 64], P('expert', 'shard'), may hold values from 100 to 897
Outputs:
- new_slow: float32 [8, 1, 64, 14336], P('expert', None, None, 'shard')
- reset_fast: bfloat16 [8, 1, 64, 14336], P('expert')
All inputs are finite; a program needn't handle non-finite values.
Results may differ from a plain program's by a relative error of at most 0.001.
Values may be sent and summed in bfloat16 or wider, within the bound.
No kernel may reach another device: no remote copies, remote signals or barrier semaphores. Data moves between devices by JAX's collectives and lax.ppermute only.
A program may use at most 64 MiB of HBM per device.

v0:
```python
import jax
import jax.numpy as jnp
from jax import lax
from jax.sharding import Mesh
from jax.sharding import PartitionSpec as P

SHARD = ("shard_0", "shard_1", "shard_2")
outer_rate = 0.7


def copy_for_each(shard, axis):
    copies = jnp.broadcast_to(shard, (lax.axis_size(axis), *shard.shape))
    return lax.all_to_all(copies, axis, split_axis=0, concat_axis=0, tiled=True)


def over_copies(shard, axis):
    return copy_for_each(shard, axis).sum(axis=0)


def in_one(arrays, axis):
    ends = [0]
    for a in arrays:
        ends.append(ends[-1] + a.size)
    total = over_copies(jnp.concatenate([a.ravel() for a in arrays]), axis)
    return tuple((total[b:e].reshape(a.shape) for a, b, e in zip(arrays, ends, ends[1:])))


def own_block(pieces, axes, turns):
    shape = [lax.axis_size(a) for a in axes]
    pieces = pieces.reshape(*shape, *pieces.shape[1:])
    pieces = pieces.transpose(*turns, *range(len(axes), pieces.ndim))
    pieces = pieces.reshape(-1, *pieces.shape[len(axes) :])
    for k in turns:
        pieces = lax.psum_scatter(pieces, axes[k], scatter_dimension=0, tiled=True)
    return pieces[0]


def cut_along(shard, dim, size):
    shape = shard.shape
    pieces = shard.reshape(*shape[:dim], size, shape[dim] // size, *shape[dim + 1 :])
    return jnp.moveaxis(pieces, dim, 0)


def scatter_axes(shard, axes, turns, dim):
    size = lax.axis_size(axes)
    return own_block(cut_along(shard, dim, size), axes, turns)


def laid_out(pieces, dim):
    pieces = jnp.moveaxis(pieces, 0, dim)
    shape = pieces.shape
    return pieces.reshape(*shape[:dim], shape[dim] * shape[dim + 1], *shape[dim + 2 :])


def stacked_from(shard, axes, turns):
    pieces = shard[None]
    for k in turns:
        pieces = lax.all_gather(pieces, axes[k], axis=0, tiled=True)
    held = [lax.axis_size(axes[k]) for k in reversed(turns)]
    pieces = pieces.reshape(*held, *shard.shape)
    turned = sorted(range(len(turns)), key=lambda place: turns[len(turns) - 1 - place])
    return pieces.transpose(*turned, *range(len(turns), pieces.ndim)).reshape(-1, *shard.shape)


def gather_axes(shard, axes, turns, dim):
    return laid_out(stacked_from(shard, axes, turns), dim)


def shards(fast_weights, slow_weights, step_counts, token_counts):
    tokens = token_counts.astype(jnp.float32)[0, 0]
    steps = step_counts.astype(jnp.float32)[0, 0]
    share = tokens / steps
    work = tokens * steps
    groups = lax.axis_size("expert")
    tok_e, work_e, qsum = in_one((tokens, work, share), SHARD)
    total = over_copies(tok_e, "expert")
    rate = outer_rate * groups * work_e / (tok_e * total)
    weighted = share * fast_weights[0, 0].astype(jnp.float32)
    slow_part = slow_weights[0]
    mixed = scatter_axes(weighted, SHARD, (2, 1, 0), 2)
    new_slow = slow_part + rate * (mixed - qsum * slow_part)
    reset = gather_axes(new_slow.astype(jnp.bfloat16), SHARD, (0, 1, 2), 2)
    return (new_slow[None], reset[None])


def solution(mesh):
    torus = Mesh(
        mesh.devices.reshape(mesh.shape["expert"], 2, 16, 2),
        ("expert", "shard_0", "shard_1", "shard_2"),
    )
    placed = (
        P("expert", SHARD, None, None, None),
        P("expert", None, None, SHARD),
        P("expert", SHARD),
        P("expert", SHARD),
    )
    return jax.shard_map(
        shards,
        mesh=torus,
        in_specs=placed,
        out_specs=(P("expert", None, None, SHARD), P("expert", None, None, None)),
        check_vma=False,
    )
```

profile of v0, /device:TPU:1, one launch (start us, length us, event | category | flops | bytes accessed | tf_op | source)
XLA Modules:
  0.0 242.1 jit_solution(16552391406660231986)
XLA Ops:
  7.2 0.0 reduce-scatter.4.cloned.1.call-start
  8.5 3.6 %convert_multiply_fusion = f32[1,1,1,64,14336]{4,3,2,1,0:T(8,128)} fusion(bf16[1,1,1,64,14336]{4,3,2,1,0:T(8,128)(2,1)} %param.4, f32[]{:T(128)} %bitcast.6), kind=kLoop, calls=%fused_computation | loop fusion | flops 1835008 | bytes 5505028 | tf_op jit(solution)/shard_map/mul | solution.py:78
  12.1 5.7 %mul.52 = f32[1,64,64,224]{3,2,1,0:T(8,128)} reshape(f32[1,1,1,64,14336]{4,3,2,1,0:T(8,128)} %convert_multiply_fusion) | data formatting | bytes 7340032 | tf_op jit(solution)/shard_map/mul | solution.py:78
  17.8 4.6 %copy.61 = f32[64,1,64,224]{3,2,0,1:T(8,128)S(1)} copy(f32[64,1,64,224]{3,0,2,1:T(8,128)} %bitcast.41) | data formatting | bytes 7340032 | tf_op jit(solution)/shard_map/transpose | solution.py:41
  22.5 2.2 copy.62
  24.7 0.0 reduce-scatter.6.cloned.1.call-start
  24.8 29.3 %reduce-scatter.4.cloned.1.call-done = f32[32,1,64,224]{3,2,0,1:T(8,128)} async-done(((f32[64,1,64,224]{3,2,0,1:T(8,128)}), f32[32,1,64,224]{3,2,0,1:T(8,128)}) %reduce-scatter.4.cloned.1.call-update) | async-done | bytes 1835024 | tf_op jit(solution)/shard_map/reduce_scatter | solution.py:34
  54.1 0.0 reduce-scatter.8.cloned.1.call-start
  54.1 66.1 %reduce-scatter.6.cloned.1.call-done = f32[2,1,64,224]{3,2,0,1:T(8,128)} async-done(((f32[32,1,64,224]{3,2,0,1:T(8,128)}), f32[2,1,64,224]{3,2,0,1:T(8,128)}) %reduce-scatter.6.cloned.1.call-update) | async-done | bytes 114704 | tf_op jit(solution)/shard_map/reduce_scatter | solution.py:34
  120.2 0.1 pad_maximum_fusion
  120.3 37.2 %all_to_all.12 = f32[64,1,3]{2,1,0:T(1,128)S(1)} all-to-all(f32[64,1,3]{2,1,0:T(1,128)S(1)} %broadcast_in_dim.8), channel_id=1, replica_groups=mesh['expert'=8,'shard_0'=2,'shard_1'=16,'shard_2'=2] {'shard_0','shard_..., dimensions={0} | all-to-all | bytes 1536 | tf_op jit(solution)/shard_map/all_to_all | solution.py:13
  157.5 0.1 reduce_sum.18
  157.5 0.6 fusion.3
  158.2 1.2 broadcast_in_dim.9
  159.4 4.1 %all-to-all-start.1 = ((f32[8,1,1]{2,1,0:T(1,128)}), f32[8,1,1]{2,1,0:T(1,128)S(1)}, u32[]{:S(2)}, u32[]{:S(2)}) async-start(f32[8,1,1]{2,1,0:T(1,128)} %broadcast_in_dim.9), calls=%async_computation.1 | async-start | bytes 8192 | tf_op jit(solution)/shard_map/all_to_all | solution.py:13
  164.2 4.3 %all-to-all-done.1 = f32[8,1,1]{2,1,0:T(1,128)S(1)} async-done(((f32[8,1,1]{2,1,0:T(1,128)}), f32[8,1,1]{2,1,0:T(1,128)S(1)}, u32[]{:S(2)}, u32[]{:S(2)}) %all-to-all-start.1) | async-done | bytes 64 | tf_op jit(solution)/shard_map/all_to_all | solution.py:13
  168.4 0.6 reduce_sum.19
  170.4 2.1 convert_bitcast_fusion
  172.5 4.9 %all_gather.9 = bf16[2,1,64,224]{3,2,1,0:T(8,128)(2,1)S(1)} all-gather(bf16[1,1,64,224]{3,2,1,0:T(8,128)(2,1)S(1)} %get-tuple-element.18), channel_id=1, replica_groups=mesh['expert'=8,'shard_0'=2,'shard_1'=16,'shard_2'=2] {'shard_0'}, dimensions={0}, use_global_device_ids=true | all-gather | bytes 86016 | tf_op jit(solution)/shard_map/all_gather | solution.py:58
  177.4 27.9 %all_gather.10 = bf16[32,1,64,224]{3,2,1,0:T(8,128)(2,1)} all-gather(bf16[2,1,64,224]{3,2,1,0:T(8,128)(2,1)S(1)} %all_gather.9), channel_id=1, replica_groups=mesh['expert'=8,'shard_0'=2,'shard_1'=16,'shard_2'=2] {'shard_1'}, dimensions={0}, use_global_device_ids=true | all-gather | bytes 974848 | tf_op jit(solution)/shard_map/all_gather | solution.py:58
  205.4 22.6 %all-gather.2.cloned.1.call-done = bf16[64,1,64,224]{3,2,1,0:T(8,128)(2,1)} async-done(((bf16[32,1,64,224]{3,2,1,0:T(8,128)(2,1)}), bf16[64,1,64,224]{3,2,1,0:T(8,128)(2,1)}) %all-gather.2.cloned.1.call-update) | async-done | bytes 1835024 | tf_op jit(solution)/shard_map/all_gather | solution.py:58
  228.0 1.7 copy.66
  229.7 1.2 copy.67
  230.9 4.7 %broadcast_in_dim_reshape.3 = bf16[1,1,64,14336]{3,2,1,0:T(8,128)(2,1)} reshape(bf16[1,64,64,224]{3,2,1,0:T(8,128)(2,1)S(1)} %copy.67) | data formatting | bytes 3670016 | tf_op jit(solution)/shard_map/broadcast_in_dim;reshape | solution.py:83
  (9 shorter events, 0.2 us)
Async XLA Ops:
  7.2 46.9 %reduce-scatter.4.cloned.1.call-start = ((), (), s32[]{:S(2)}) async-start(), calls=%async_computation.5 | async-start | bytes 6291456 | tf_op jit(solution)/shard_map/reduce_scatter | solution.py:34
  24.7 145.7 %copy-start = (f32[1,1,64,224]{3,2,1,0:T(8,128)S(1)}, f32[1,1,64,224]{3,2,1,0:T(8,128)}, u32[]{:S(2)}) copy-start(f32[1,1,64,224]{3,2,1,0:T(8,128)} %param.5) | copy-start | bytes 172036
  24.7 95.4 %reduce-scatter.6.cloned.1.call-start = ((), (), s32[]{:S(2)}) async-start(), calls=%async_computation.6 | async-start | bytes 2228224 | tf_op jit(solution)/shard_map/reduce_scatter | solution.py:34
  54.1 116.3 %reduce-scatter.8.cloned.1.call-start = ((), (), s32[]{:S(2)}) async-start(), calls=%async_computation.7 | async-start | bytes 196608 | tf_op jit(solution)/shard_map/reduce_scatter | solution.py:34
  159.4 9.0 %all-to-all-start.1 = ((f32[8,1,1]{2,1,0:T(1,128)}), f32[8,1,1]{2,1,0:T(1,128)S(1)}, u32[]{:S(2)}, u32[]{:S(2)}) async-start(f32[8,1,1]{2,1,0:T(1,128)} %broadcast_in_dim.9), calls=%async_computation.1 | async-start | bytes 8192 | tf_op jit(solution)/shard_map/all_to_all | solution.py:13
  163.5 64.5 %all-gather.2.cloned.1.call-start = ((), (), s32[]{:S(2)}) async-start(), calls=%async_computation.8 | async-start | bytes 3145728 | tf_op jit(solution)/shard_map/all_gather | solution.py:58
Sparse Core Ops, SparseCore 0:
  24.8 29.1 reduce-scatter.3
  57.1 63.0 reduce-scatter.5
  123.1 30.0 reduce-scatter.7
  205.5 22.4 all-gather.1
where the time goes:
time: 243 us; the launch traced here: 242 us
  waiting for transfers between devices  122 us (50%)
  blocking collectives  70 us (29%)
  local copies, waits for them, and re-layouts  22.1 us (9%)
  between operations  17.1 us (7%)
  other arithmetic  6.46 us (3%)
  starting transfers between devices  4.21 us (2%)
    reduce_scatter x3, waiting for transfers between devices, own_block(): pieces = lax.psum_scatter(pieces, axes[k], scatter_dimension=0, tiled=True)  95.3 us
    all_to_all x1, blocking collectives, copy_for_each(): return lax.all_to_all(copies, axis, split_axis=0, concat_axis=0, tiled=True)  37.2 us
    all_gather x2, blocking collectives, stacked_from(): pieces = lax.all_gather(pieces, axes[k], axis=0, tiled=True)  32.8 us
    all_gather x1, waiting for transfers between devices, stacked_from(): pieces = lax.all_gather(pieces, axes[k], axis=0, tiled=True)  22.6 us
    mul x1, local copies, waits for them, and re-layouts, shards(): weighted = share * fast_weights[0, 0].astype(jnp.float32)  5.72 us
  transfers between devices with their start and end apart: 5, of which 4 were waited for; matrix products, arithmetic and copies ran while one was open for 1% of the time, Pallas kernels for 0%

commit v1 on v0

--- a/solution.py
+++ b/solution.py
@@ -55,7 +55,9 @@
 def stacked_from(shard, axes, turns):
     pieces = shard[None]
     for k in turns:
-        pieces = lax.all_gather(pieces, axes[k], axis=0, tiled=True)
+        pieces = jnp.concatenate(
+            lax.all_to_all(jnp.stack([pieces] * lax.axis_size(axes[k])), axes[k], 0, 0), axis=0
+        )
     held = [lax.axis_size(axes[k]) for k in reversed(turns)]
     pieces = pieces.reshape(*held, *shard.shape)
     turned = sorted(range(len(turns)), key=lambda place: turns[len(turns) - 1 - place])

time: 243 us -> 252 us (1.037)
  waiting for transfers between devices: 122 us -> 143 us
  blocking collectives: 70 us -> 54.7 us
  starting transfers between devices: 4.21 us -> 7.82 us
    all_to_all x0 -> x1, waiting for transfers between devices: none -> 42.8 us  [stacked_from(): lax.all_to_all(jnp.stack([pieces] * lax.axis_size(axes[k])), axes[k], 0, 0)]
    all_gather x2 -> x0, blocking collectives: 32.8 us -> none  [stacked_from(): pieces = lax.all_gather(pieces, axes[k], axis=0, tiled=True)]
    all_gather x1 -> x0, waiting for transfers between devices: 22.6 us -> none  [stacked_from(): pieces = lax.all_gather(pieces, axes[k], axis=0, tiled=True)]
    all_to_all x0 -> x2, blocking collectives: none -> 17.5 us  [stacked_from(): lax.all_to_all(jnp.stack([pieces] * lax.axis_size(axes[k])), axes[k], 0, 0)]
    all_to_all x0 -> x1, starting transfers between devices: none -> 3.66 us  [stacked_from(): lax.all_to_all(jnp.stack([pieces] * lax.axis_size(axes[k])), axes[k], 0, 0)]
  transfers between devices with their start and end apart: 5 -> 5, of which waited for: 4 -> 4; matrix products, arithmetic and copies ran while one was open for 1% -> 2% of each run, Pallas kernels for 0% -> 0%
where the time goes in v1:
time: 252 us; the launch traced here: 251 us
  waiting for transfers between devices  143 us (57%)
  blocking collectives  54.7 us (22%)
  local copies, waits for them, and re-layouts  21.7 us (9%)
  between operations  17.1 us (7%)
  starting transfers between devices  7.82 us (3%)
  other arithmetic  7.42 us (3%)
    reduce_scatter x3, waiting for transfers between devices, own_block(): pieces = lax.psum_scatter(pieces, axes[k], scatter_dimension=0, tiled=True)  95.3 us
    all_to_all x1, waiting for transfers between devices, stacked_from(): lax.all_to_all(jnp.stack([pieces] * lax.axis_size(axes[k])), axes[k], 0, 0)  42.8 us
    all_to_all x1, blocking collectives, copy_for_each(): return lax.all_to_all(copies, axis, split_axis=0, concat_axis=0, tiled=True)  37.2 us
    all_to_all x2, blocking collectives, stacked_from(): lax.all_to_all(jnp.stack([pieces] * lax.axis_size(axes[k])), axes[k], 0, 0)  17.5 us
    mul x1, local copies, waits for them, and re-layouts, shards(): weighted = share * fast_weights[0, 0].astype(jnp.float32)  5.72 us
  transfers between devices with their start and end apart: 5, of which 4 were waited for; matrix products, arithmetic and copies ran while one was open for 2% of the time, Pallas kernels for 0%

profile of v1, /device:TPU:1, one launch (start us, length us, event | category | flops | bytes accessed | tf_op | source)
XLA Modules:
  0.0 251.2 jit_solution(7856411933699216469)
XLA Ops:
  8.5 3.6 %convert_multiply_fusion = f32[1,1,1,64,14336]{4,3,2,1,0:T(8,128)} fusion(bf16[1,1,1,64,14336]{4,3,2,1,0:T(8,128)(2,1)} %param.4, f32[]{:T(128)} %bitcast.6), kind=kLoop, calls=%fused_computation | loop fusion | flops 1835008 | bytes 5505028 | tf_op jit(solution)/shard_map/mul | solution.py:80
  12.1 5.7 %mul.72 = f32[1,64,64,224]{3,2,1,0:T(8,128)} reshape(f32[1,1,1,64,14336]{4,3,2,1,0:T(8,128)} %convert_multiply_fusion) | data formatting | bytes 7340032 | tf_op jit(solution)/shard_map/mul | solution.py:80
  17.9 4.6 %copy.44 = f32[64,1,64,224]{3,2,0,1:T(8,128)S(1)} copy(f32[64,1,64,224]{3,0,2,1:T(8,128)} %bitcast.52) | data formatting | bytes 7340032 | tf_op jit(solution)/shard_map/transpose | solution.py:41
  22.5 2.2 copy.45
  24.8 29.2 %reduce-scatter.4.cloned.1.call-done = f32[32,1,64,224]{3,2,0,1:T(8,128)} async-done(((f32[64,1,64,224]{3,2,0,1:T(8,128)}), f32[32,1,64,224]{3,2,0,1:T(8,128)}) %reduce-scatter.4.cloned.1.call-update) | async-done | bytes 1835024 | tf_op jit(solution)/shard_map/reduce_scatter | solution.py:34
  54.1 66.1 %reduce-scatter.6.cloned.1.call-done = f32[2,1,64,224]{3,2,0,1:T(8,128)} async-done(((f32[32,1,64,224]{3,2,0,1:T(8,128)}), f32[2,1,64,224]{3,2,0,1:T(8,128)}) %reduce-scatter.6.cloned.1.call-update) | async-done | bytes 114704 | tf_op jit(solution)/shard_map/reduce_scatter | solution.py:34
  120.3 37.2 %all_to_all.27 = f32[64,1,3]{2,1,0:T(1,128)S(1)} all-to-all(f32[64,1,3]{2,1,0:T(1,128)S(1)} %broadcast_in_dim.7), channel_id=1, replica_groups=mesh['expert'=8,'shard_0'=2,'shard_1'=16,'shard_2'=2] {'shard_0','shard_..., dimensions={0} | all-to-all | bytes 1536 | tf_op jit(solution)/shard_map/all_to_all | solution.py:13
  157.5 0.1 reduce_sum.18
  157.6 0.6 fusion.6
  158.2 1.2 broadcast_in_dim.8
  159.4 4.1 %all-to-all-start.1 = ((f32[8,1,1]{2,1,0:T(1,128)}), f32[8,1,1]{2,1,0:T(1,128)S(1)}, u32[]{:S(2)}, u32[]{:S(2)}) async-start(f32[8,1,1]{2,1,0:T(1,128)} %broadcast_in_dim.8), calls=%async_computation.1 | async-start | bytes 8192 | tf_op jit(solution)/shard_map/all_to_all | solution.py:13
  164.1 4.3 %all-to-all-done.1 = f32[8,1,1]{2,1,0:T(1,128)S(1)} async-done(((f32[8,1,1]{2,1,0:T(1,128)}), f32[8,1,1]{2,1,0:T(1,128)S(1)}, u32[]{:S(2)}, u32[]{:S(2)}) %all-to-all-start.1) | async-done | bytes 64 | tf_op jit(solution)/shard_map/all_to_all | solution.py:13
  168.4 0.6 reduce_sum.19
  170.4 1.4 fusion.2
  171.9 6.9 %all_to_all.28 = bf16[2,1,1,64,224]{4,3,2,1,0:T(8,128)(2,1)S(1)} all-to-all(bf16[2,1,1,64,224]{4,3,2,1,0:T(8,128)(2,1)S(1)} %pad_maximum_fusion.1), channel_id=1, replica_groups=mesh['expert'=8,'shard_0'=2,'shard_1'=16,'shard_2'=2] {'shard_0'}, dimensions={0} | all-to-all | bytes 114688 | tf_op jit(solution)/shard_map/all_to_all | solution.py:59
  178.7 1.1 stack.10
  179.8 3.7 %all-to-all-start.3 = ((bf16[16,2,1,64,224]{4,3,1,2,0:T(8,128)(2,1)}), bf16[16,2,1,64,224]{4,3,1,2,0:T(8,128)(2,1)S(1)}, u32[]{:S(2)}, u32[]{:S(2)}) async-start(bf16[16,2,1,64,224]{4,3,1,2,0:T(8,128)(2,1)} %stack.10), calls=%async_computation.6 | async-start | bytes 2097152 | tf_op jit(solution)/shard_map/all_to_all | solution.py:59
  183.5 1.2 fusion.3
  184.7 42.8 %all-to-all-done.3 = bf16[16,2,1,64,224]{4,3,1,2,0:T(8,128)(2,1)S(1)} async-done(((bf16[16,2,1,64,224]{4,3,1,2,0:T(8,128)(2,1)}), bf16[16,2,1,64,224]{4,3,1,2,0:T(8,128)(2,1)S(1)}, u32[]{:S(2)}, u32[]{:S(2)}) %all-to-all-start.3) | async-done | bytes 917536 | tf_op jit(solution)/shard_map/all_to_all | solution.py:59
  227.5 0.4 pad_maximum_fusion
  227.9 10.7 %all_to_all.29 = bf16[2,32,1,64,224]{4,3,1,2,0:T(8,128)(2,1)S(1)} all-to-all(bf16[2,32,1,64,224]{4,3,1,2,0:T(8,128)(2,1)S(1)} %pad_maximum_fusion), channel_id=1, replica_groups=mesh['expert'=8,'shard_0'=2,'shard_1'=16,'shard_2'=2] {'shard_2'}, dimensions={0} | all-to-all | bytes 3670016 | tf_op jit(solution)/shard_map/all_to_all | solution.py:59
  238.6 0.2 copy.48
  238.8 1.2 copy.49
  240.0 4.7 %broadcast_in_dim_reshape.3 = bf16[1,1,64,14336]{3,2,1,0:T(8,128)(2,1)} reshape(bf16[1,64,64,224]{3,2,1,0:T(8,128)(2,1)S(1)} %copy.49) | data formatting | bytes 3670016 | tf_op jit(solution)/shard_map/broadcast_in_dim;reshape | solution.py:85
  (14 shorter events, 0.3 us)
Async XLA Ops:
  7.2 46.9 %reduce-scatter.4.cloned.1.call-start = ((), (), s32[]{:S(2)}) async-start(), calls=%async_computation.8 | async-start | bytes 6291456 | tf_op jit(solution)/shard_map/reduce_scatter | solution.py:34
  24.7 145.7 %copy-start = (f32[1,1,64,224]{3,2,1,0:T(8,128)S(1)}, f32[1,1,64,224]{3,2,1,0:T(8,128)}, u32[]{:S(2)}) copy-start(f32[1,1,64,224]{3,2,1,0:T(8,128)} %param.5) | copy-start | bytes 172036
  24.7 95.4 %reduce-scatter.6.cloned.1.call-start = ((), (), s32[]{:S(2)}) async-start(), calls=%async_computation.9 | async-start | bytes 2228224 | tf_op jit(solution)/shard_map/reduce_scatter | solution.py:34
  54.1 116.3 %reduce-scatter.8.cloned.1.call-start = ((), (), s32[]{:S(2)}) async-start(), calls=%async_computation.10 | async-start | bytes 196608 | tf_op jit(solution)/shard_map/reduce_scatter | solution.py:34
  159.4 9.0 %all-to-all-start.1 = ((f32[8,1,1]{2,1,0:T(1,128)}), f32[8,1,1]{2,1,0:T(1,128)S(1)}, u32[]{:S(2)}, u32[]{:S(2)}) async-start(f32[8,1,1]{2,1,0:T(1,128)} %broadcast_in_dim.8), calls=%async_computation.1 | async-start | bytes 8192 | tf_op jit(solution)/shard_map/all_to_all | solution.py:13
  170.4 13.1 %copy-start.1 = (f32[1,1,64,224]{3,2,0,1:T(8,128)S(1)}, f32[1,1,64,224]{3,2,0,1:T(8,128)}, u32[]{:S(2)}) copy-start(f32[1,1,64,224]{3,2,0,1:T(8,128)} %reduce-scatter.8.cloned.1.call-done) | copy-start | bytes 172036
  179.8 47.7 %all-to-all-start.3 = ((bf16[16,2,1,64,224]{4,3,1,2,0:T(8,128)(2,1)}), bf16[16,2,1,64,224]{4,3,1,2,0:T(8,128)(2,1)S(1)}, u32[]{:S(2)}, u32[]{:S(2)}) async-start(bf16[16,2,1,64,224]{4,3,1,2,0:T(8,128)(2,1)} %stack.10), calls=%async_computation.6 | async-start | bytes 2097152 | tf_op jit(solution)/shard_map/all_to_all | solution.py:59
Sparse Core Ops, SparseCore 0:
  24.9 29.1 reduce-scatter.3
  57.1 63.0 reduce-scatter.5
  123.1 30.0 reduce-scatter.7
